TPU v7x, 32 devices: a whole 2x2x4 slice. The times are simulated.
32 devices in a mesh: groups: 2 (over y), hist: 2 (over x), rows: 4 (over z), cols: 2 (over core).
Axes of the slice: x: 2, y: 2, z: 4, core: 2. Of those that a mesh axis runs over, the one named last changes fastest.
Arguments:
- hists: float32 [2, 1024, 4096], P('hist', ('groups', 'rows'), 'cols'), parts along dimension 1, may hold values from 0.2 to 2000, as said below
- log_scaling_fields: float32 [2, 1024, 4096], P('hist', ('groups', 'rows'), 'cols'), parts along dimension 1, may hold values from -1 to 1
- histogram_weight_list: float32 [2], replicated, may hold values from 0.25 to 4
Outputs:
- barycenter: float32 [1024, 4096], P(('groups', 'rows'), 'cols'), parts along dimension 0
- new_logs: float32 [2, 1024, 4096], P('hist', ('groups', 'rows'), 'cols'), parts along dimension 1
There are 2 independent parts, one for each index of `groups`. A program takes and returns all parts, laid end to end along the dimension named above; an argument that names none is the same for every part. Nothing has to cross between parts.
Inputs may be any that keep to these rules, and one draw needn't show every extreme that they name: `hists`: every entry is positive.
All inputs are finite; a program needn't handle non-finite values.
Results may differ from a plain program's by a relative error of at most 0.00021.
Values sent between devices are 32-bit elements; how exact they have to be, the bound alone decides.
A program may use at most 64 MiB of HBM per device.

v0:
```python
import jax
import jax.numpy as jnp
from jax import lax
from jax.sharding import PartitionSpec as P

HALF = 32
kernel_sigma = 16.0


def padded_2(cells, sides, width):
    for axis, dim in sides:
        count = lax.axis_size(axis)
        ends = count - 1
        head = lax.slice_in_dim(cells, 0, width, axis=dim)
        tail = lax.slice_in_dim(cells, cells.shape[dim] - width, cells.shape[dim], axis=dim)
        cells = jnp.concatenate(
            [
                lax.ppermute(tail, axis, [(i, (i + 1) % count) for i in range(ends)]),
                cells,
                lax.ppermute(head, axis, [((i + 1) % count, i) for i in range(ends)]),
            ],
            axis=dim,
        )
    return cells


def band_matrix(width_out):
    shape_full = (width_out + 2 * HALF, width_out)
    rows_in = lax.broadcasted_iota(jnp.int32, shape_full, 0)
    cols_out = lax.broadcasted_iota(jnp.int32, shape_full, 1)
    offsets = (rows_in - cols_out - HALF).astype(jnp.float32)
    tap_offsets = jnp.arange(-HALF, HALF + 1).astype(jnp.float32)
    tap_total = jnp.sum(jnp.exp(-tap_offsets * tap_offsets / (2.0 * kernel_sigma * kernel_sigma)))
    entries = jnp.exp(-offsets * offsets / (2.0 * kernel_sigma * kernel_sigma)) / tap_total
    return jnp.where(jnp.abs(offsets) <= HALF, entries, 0.0)


def column_pass(padded, width_out):
    block_list = []
    for offset in range(0, width_out, 256):
        span_cols = min(256, width_out - offset)
        window = padded[:, offset : offset + span_cols + 2 * HALF]
        block_list.append(
            jnp.dot(
                window,
                band_matrix(span_cols),
                precision=lax.Precision.HIGHEST,
                preferred_element_type=jnp.float32,
            )
        )
    return jnp.concatenate(block_list, axis=1)


def row_pass(across, height_out):
    return jnp.dot(
        band_matrix(height_out).T,
        across,
        precision=lax.Precision.HIGHEST,
        preferred_element_type=jnp.float32,
    )


def blurred_patch(padded, height_out, width_out):
    return row_pass(column_pass(padded, width_out), height_out)


def neighbor_total(values):
    return padded_2(values, (("rows", 0), ("cols", 1)), HALF)


def body(hists, log_scaling_fields, histogram_weight_list):
    masses = hists[0]
    local_log_values = log_scaling_fields[0]
    patch_height = masses.shape[0]
    patch_width = masses.shape[1]
    scaling_fields = jnp.exp(local_log_values)
    blurred_vertical = blurred_patch(neighbor_total(scaling_fields), patch_height, patch_width)
    ratios = masses / blurred_vertical
    smooth_u = blurred_patch(neighbor_total(ratios), patch_height, patch_width)
    log_blurred = jnp.log(smooth_u)
    log_portions = local_log_values + log_blurred
    position = lax.axis_index("hist")
    own_pick = lax.broadcasted_iota(jnp.int32, histogram_weight_list.shape, 0) == position
    own_weight = jnp.sum(jnp.where(own_pick, histogram_weight_list, 0.0)) / jnp.sum(
        histogram_weight_list
    )
    weighted = own_weight * log_portions
    cell_count = patch_height * lax.axis_size("rows") * patch_width * lax.axis_size("cols")
    log_mean = lax.psum(weighted, "hist")
    mean_field = jnp.exp(log_mean)
    total_mass = lax.psum(jnp.sum(mean_field), ("rows", "cols"))
    barycenter = mean_field * (cell_count / total_mass)
    new_logs = jnp.log(barycenter) - log_blurred
    return (barycenter, new_logs[None])


def solution(mesh):
    return jax.shard_map(
        body,
        mesh=mesh,
        in_specs=(
            P("hist", ("groups", "rows"), "cols"),
            P("hist", ("groups", "rows"), "cols"),
            P(),
        ),
        out_specs=(P(("groups", "rows"), "cols"), P("hist", ("groups", "rows"), "cols")),
        check_vma=False,
    )
```

profile of v0, /device:TPU:0, one launch (start us, length us, event | category | flops | bytes accessed | tf_op | source)
XLA Modules:
  0.0 137.3 jit_solution(3415353745641295112)
XLA Ops:
  7.2 0.0 all-reduce.2.cloned.1.call-start
  7.2 1.4 %bitcast_exponential_fusion = f32[128,2048]{1,0:T(8,128)S(1)} fusion(f32[1,128,2048]{2,1,0:T(8,128)} %param.4), kind=kLoop, calls=%fused_computation.21 | loop fusion | bytes 2097152 | tf_op jit(solution)/shard_map/exp | solution.py:76
  8.6 5.0 %collective-permute-start = (f32[32,2048]{1,0:T(8,128)S(1)}, f32[32,2048]{1,0:T(8,128)S(1)}, u32[]{:S(2)}, u32[]{:S(2)}) collective-permute-start(f32[32,2048]{1,0:T(8,128)S(1)} %get-tuple-element.12), channel_id=1, source_target_pairs={{0,2},{2,4},{4,6},{1,3},{3,5},{5,7},{8,10},{10,12},{12,14},{9,11},... | collective-permute-start | bytes 786440 | tf_op jit(solution)/shard_map/ppermute | solution.py:18
  13.6 1.3 collective-permute-start.1
  14.9 0.6 fusion.45
  15.6 3.6 %collective-permute-done = f32[32,2048]{1,0:T(8,128)S(1)} collective-permute-done((f32[32,2048]{1,0:T(8,128)S(1)}, f32[32,2048]{1,0:T(8,128)S(1)}, u32[]{:S(2)}, u32[]{:S(2)}) %collective-permute-start) | collective-permute-done | bytes 262176 | tf_op jit(solution)/shard_map/ppermute | solution.py:18
  19.2 4.1 %collective-permute-done.1 = f32[32,2048]{1,0:T(8,128)S(1)} collective-permute-done((f32[32,2048]{1,0:T(8,128)S(1)}, f32[32,2048]{1,0:T(8,128)S(1)}, u32[]{:S(2)}, u32[]{:S(2)}) %collective-permute-start.1) | collective-permute-done | bytes 262176 | tf_op jit(solution)/shard_map/ppermute | solution.py:20
  23.3 0.1 pad_maximum_fusion.28
  23.4 1.3 collective-permute-start.2
  24.7 1.3 collective-permute-start.3
  26.0 0.1 pad_maximum_fusion
  26.1 0.0 collective-permute-done.2
  26.1 1.2 convolution_dynamic-update-slice_fusion.15
  27.4 1.2 convolution_dynamic-update-slice_fusion.14
  28.6 1.2 convolution_dynamic-update-slice_fusion.13
  29.9 1.2 convolution_dynamic-update-slice_fusion.12
  31.1 1.2 convolution_dynamic-update-slice_fusion.11
  32.3 1.2 convolution_dynamic-update-slice_fusion.10
  33.6 1.2 convolution_dynamic-update-slice_fusion.9
  34.8 0.0 copy-start.3
  34.8 0.0 collective-permute-done.3
  34.8 1.3 convolution_dynamic-update-slice_fusion.8
  36.2 0.0 copy-done.3
  36.2 0.0 copy-start.2
  36.2 1.8 %convolution_divide_fusion = f32[128,2048]{1,0:T(8,128)S(1)} fusion(f32[192,2048]{1,0:T(8,128)S(1)} %convolution_dynamic-update-slice_fusion.8, f32[1,128,2048]{2,1,0:T(8,128)S(1)} %copy-done.3, f32[]{:T(128)} %fusion.45), kind=kOutput, calls=%fused_computation.1 | convolution fusion | flops 604487680 | bytes 3670020 | tf_op jit(solution)/shard_map/dot_general | solution.py:55
  38.0 3.5 %collective-permute-start.4 = (f32[32,2048]{1,0:T(8,128)S(1)}, f32[32,2048]{1,0:T(8,128)S(1)}, u32[]{:S(2)}, u32[]{:S(2)}) collective-permute-start(f32[32,2048]{1,0:T(8,128)S(1)} %get-tuple-element.10), channel_id=1, source_target_pairs={{0,2},{2,4},{4,6},{1,3},{3,5},{5,7},{8,10},{10,12},{12,14},{9,11},... | collective-permute-start | bytes 786440 | tf_op jit(solution)/shard_map/ppermute | solution.py:18
  41.5 1.3 collective-permute-start.5
  42.8 0.0 copy-done.2
  42.8 0.6 fusion.123
  44.8 3.2 %collective-permute-done.4 = f32[32,2048]{1,0:T(8,128)S(1)} collective-permute-done((f32[32,2048]{1,0:T(8,128)S(1)}, f32[32,2048]{1,0:T(8,128)S(1)}, u32[]{:S(2)}, u32[]{:S(2)}) %collective-permute-start.4) | collective-permute-done | bytes 262176 | tf_op jit(solution)/shard_map/ppermute | solution.py:18
  48.0 4.5 %collective-permute-done.5 = f32[32,2048]{1,0:T(8,128)S(1)} collective-permute-done((f32[32,2048]{1,0:T(8,128)S(1)}, f32[32,2048]{1,0:T(8,128)S(1)}, u32[]{:S(2)}, u32[]{:S(2)}) %collective-permute-start.5) | collective-permute-done | bytes 262176 | tf_op jit(solution)/shard_map/ppermute | solution.py:20
  52.5 0.1 pad_maximum_fusion.26
  52.6 1.9 %collective-permute-start.6 = (f32[192,32]{1,0:T(8,128)S(1)}, f32[192,32]{1,0:T(8,128)S(1)}, u32[]{:S(2)}, u32[]{:S(2)}) collective-permute-start(f32[192,32]{1,0:T(8,128)S(1)} %get-tuple-element.7), channel_id=1, source_target_pairs={{0,1},{2,3},{4,5},{6,7},{8,9},{10,11},{12,13},{14,15},{16,17},{18,... | collective-permute-start | bytes 73736 | tf_op jit(solution)/shard_map/ppermute | solution.py:18
  54.5 1.5 %collective-permute-start.7 = (f32[192,32]{1,0:T(8,128)S(1)}, f32[192,32]{1,0:T(8,128)S(1)}, u32[]{:S(2)}, u32[]{:S(2)}) collective-permute-start(f32[192,32]{1,0:T(8,128)S(1)} %get-tuple-element.6), channel_id=1, source_target_pairs={{1,0},{3,2},{5,4},{7,6},{9,8},{11,10},{13,12},{15,14},{17,16},{19,... | collective-permute-start | bytes 73736 | tf_op jit(solution)/shard_map/ppermute | solution.py:20
  55.9 0.1 pad_maximum_fusion.1
  56.1 0.0 collective-permute-done.6
  56.1 1.2 convolution_dynamic-update-slice_fusion.7
  57.3 1.2 convolution_dynamic-update-slice_fusion.6
  58.5 1.2 convolution_dynamic-update-slice_fusion.5
  59.8 1.2 convolution_dynamic-update-slice_fusion.4
  61.0 1.2 convolution_dynamic-update-slice_fusion.3
  62.3 1.2 convolution_dynamic-update-slice_fusion.2
  63.5 1.2 convolution_dynamic-update-slice_fusion.1
  64.7 0.0 copy-start
  64.7 0.0 collective-permute-done.7
  64.8 1.3 convolution_dynamic-update-slice_fusion
  66.1 0.0 copy-done
  66.1 2.8 %fusion = (f32[128,2048]{1,0:T(8,128)}, f32[128,2048]{1,0:T(8,128)S(1)}) fusion(f32[1,128,2048]{2,1,0:T(8,128)S(1)} %copy-done, f32[]{:T(128)S(6)} %div.20, f32[192,2048]{1,0:T(8,128)S(1)} %convolution_dynamic-update-slice_fusion, f32[]{:T(128)} %fusion.45), kind=kOutput, calls=%fused_computation.22 | convolution fusion | flops 604749824 | bytes 4718600 | tf_op jit(solution)/shard_map/dot_general | solution.py:55
  68.9 0.0 all-reduce.2.cloned.1.call-update
  69.0 40.2 %all-reduce.2.cloned.1.call-done = f32[128,2048]{1,0:T(8,128)} async-done(((f32[128,2048]{1,0:T(8,128)}), f32[128,2048]{1,0:T(8,128)}) %all-reduce.2.cloned.1.call-update) | async-done | bytes 1048592 | tf_op jit(solution)/shard_map/psum | solution.py:89
  109.2 0.0 copy-start.1
  109.2 2.2 %exponential_reduce_fusion = f32[]{:T(128)} fusion(f32[128,2048]{1,0:T(8,128)} %all-reduce.2.cloned.1.call-done), kind=kLoop, calls=%fused_computation.25 | loop fusion | flops 262143 | bytes 1048580 | tf_op jit(solution)/shard_map/reduce_sum | solution.py:91
  111.4 16.8 %psum.15 = f32[]{:T(128)} all-reduce(f32[]{:T(128)} %exponential_reduce_fusion), channel_id=1, replica_groups=mesh['groups'=2,'hist'=2,'rows'=4,'cols'=2] {'rows','cols'}, use_global_device_ids=true, to_apply=%region_5.6 | all-reduce | flops 1 | bytes 8 | tf_op jit(solution)/shard_map/psum | solution.py:91
  128.9 0.0 copy-done.1
  128.9 1.6 %subtract_bitcast_fusion = (f32[1,128,2048]{2,1,0:T(8,128)}, f32[128,2048]{1,0:T(8,128)}) fusion(f32[128,2048]{1,0:T(8,128)S(1)} %get-tuple-element.15, f32[]{:T(128)S(6)} %div.29, f32[128,2048]{1,0:T(8,128)S(1)} %copy-done.1), kind=kLoop, calls=%fused_computation.23 | loop fusion | flops 524288 | bytes 4194308 | tf_op jit(solution)/shard_map/broadcast_in_dim | solution.py:94
  (2 shorter events, 0.1 us)
Async XLA Ops:
  7.2 102.0 %all-reduce.2.cloned.1.call-start = ((), (), s32[]{:S(2)}) async-start(), calls=%async_computation | async-start | bytes 2097152 | tf_op jit(solution)/shard_map/psum | solution.py:89
  8.6 10.5 %collective-permute-start = (f32[32,2048]{1,0:T(8,128)S(1)}, f32[32,2048]{1,0:T(8,128)S(1)}, u32[]{:S(2)}, u32[]{:S(2)}) collective-permute-start(f32[32,2048]{1,0:T(8,128)S(1)} %get-tuple-element.12), channel_id=1, source_target_pairs={{0,2},{2,4},{4,6},{1,3},{3,5},{5,7},{8,10},{10,12},{12,14},{9,11},... | collective-permute-start | bytes 786440 | tf_op jit(solution)/shard_map/ppermute | solution.py:18
  13.6 9.7 %collective-permute-start.1 = (f32[32,2048]{1,0:T(8,128)S(1)}, f32[32,2048]{1,0:T(8,128)S(1)}, u32[]{:S(2)}, u32[]{:S(2)}) collective-permute-start(f32[32,2048]{1,0:T(8,128)S(1)} %get-tuple-element.13), channel_id=1, source_target_pairs={{2,0},{4,2},{6,4},{3,1},{5,3},{7,5},{10,8},{12,10},{14,12},{11,9},... | collective-permute-start | bytes 786440 | tf_op jit(solution)/shard_map/ppermute | solution.py:20
  23.4 2.8 %collective-permute-start.2 = (f32[192,32]{1,0:T(8,128)S(1)}, f32[192,32]{1,0:T(8,128)S(1)}, u32[]{:S(2)}, u32[]{:S(2)}) collective-permute-start(f32[192,32]{1,0:T(8,128)S(1)} %get-tuple-element.9), channel_id=1, source_target_pairs={{0,1},{2,3},{4,5},{6,7},{8,9},{10,11},{12,13},{14,15},{16,17},{18,... | collective-permute-start | bytes 73736 | tf_op jit(solution)/shard_map/ppermute | solution.py:18
  24.7 10.1 %collective-permute-start.3 = (f32[192,32]{1,0:T(8,128)S(1)}, f32[192,32]{1,0:T(8,128)S(1)}, u32[]{:S(2)}, u32[]{:S(2)}) collective-permute-start(f32[192,32]{1,0:T(8,128)S(1)} %get-tuple-element.8), channel_id=1, source_target_pairs={{1,0},{3,2},{5,4},{7,6},{9,8},{11,10},{13,12},{15,14},{17,16},{19,... | collective-permute-start | bytes 73736 | tf_op jit(solution)/shard_map/ppermute | solution.py:20
  34.8 1.4 copy-start.3
  36.2 6.6 %copy-start.2 = (f32[2]{0:T(128)S(1)}, f32[2]{0:T(128)}, u32[]{:S(2)}) copy-start(f32[2]{0:T(128)} %param.5) | copy-start | bytes 28
  38.0 10.0 %collective-permute-start.4 = (f32[32,2048]{1,0:T(8,128)S(1)}, f32[32,2048]{1,0:T(8,128)S(1)}, u32[]{:S(2)}, u32[]{:S(2)}) collective-permute-start(f32[32,2048]{1,0:T(8,128)S(1)} %get-tuple-element.10), channel_id=1, source_target_pairs={{0,2},{2,4},{4,6},{1,3},{3,5},{5,7},{8,10},{10,12},{12,14},{9,11},... | collective-permute-start | bytes 786440 | tf_op jit(solution)/shard_map/ppermute | solution.py:18
  41.5 11.0 %collective-permute-start.5 = (f32[32,2048]{1,0:T(8,128)S(1)}, f32[32,2048]{1,0:T(8,128)S(1)}, u32[]{:S(2)}, u32[]{:S(2)}) collective-permute-start(f32[32,2048]{1,0:T(8,128)S(1)} %get-tuple-element.11), channel_id=1, source_target_pairs={{2,0},{4,2},{6,4},{3,1},{5,3},{7,5},{10,8},{12,10},{14,12},{11,9},... | collective-permute-start | bytes 786440 | tf_op jit(solution)/shard_map/ppermute | solution.py:20
  52.6 3.5 %collective-permute-start.6 = (f32[192,32]{1,0:T(8,128)S(1)}, f32[192,32]{1,0:T(8,128)S(1)}, u32[]{:S(2)}, u32[]{:S(2)}) collective-permute-start(f32[192,32]{1,0:T(8,128)S(1)} %get-tuple-element.7), channel_id=1, source_target_pairs={{0,1},{2,3},{4,5},{6,7},{8,9},{10,11},{12,13},{14,15},{16,17},{18,... | collective-permute-start | bytes 73736 | tf_op jit(solution)/shard_map/ppermute | solution.py:18
  54.5 10.3 %collective-permute-start.7 = (f32[192,32]{1,0:T(8,128)S(1)}, f32[192,32]{1,0:T(8,128)S(1)}, u32[]{:S(2)}, u32[]{:S(2)}) collective-permute-start(f32[192,32]{1,0:T(8,128)S(1)} %get-tuple-element.6), channel_id=1, source_target_pairs={{1,0},{3,2},{5,4},{7,6},{9,8},{11,10},{13,12},{15,14},{17,16},{19,... | collective-permute-start | bytes 73736 | tf_op jit(solution)/shard_map/ppermute | solution.py:20
  64.7 1.4 %copy-start = (f32[1,128,2048]{2,1,0:T(8,128)S(1)}, f32[1,128,2048]{2,1,0:T(8,128)}, u32[]{:S(2)}) copy-start(f32[1,128,2048]{2,1,0:T(8,128)} %param.4) | copy-start | bytes 3145732
  109.2 19.7 %copy-start.1 = (f32[128,2048]{1,0:T(8,128)S(1)}, f32[128,2048]{1,0:T(8,128)}, u32[]{:S(2)}) copy-start(f32[128,2048]{1,0:T(8,128)} %all-reduce.2.cloned.1.call-done) | copy-start | bytes 3145732
Sparse Core Ops, SparseCore 0:
  69.1 40.0 all-reduce.1
where the time goes:
time: 138 us; the launch traced here: 137 us
  waiting for transfers between devices  55.7 us (40%)
  matrix products  24.5 us (18%)
  starting transfers between devices  17 us (12%)
  blocking collectives  16.8 us (12%)
  between operations  16.4 us (12%)
  other arithmetic  5.45 us (4%)
  local copies, waits for them, and re-layouts  1.48 us (1%)
    psum x1, waiting for transfers between devices, body(): log_mean = lax.psum(weighted, 'hist')  40.2 us
    dot_general x16, matrix products, column_pass(): jnp.dot(window, band_matrix(span_cols), precision=lax.Precision.HIGHEST,...  19.9 us
    psum x1, blocking collectives, body(): total_mass = lax.psum(jnp.sum(mean_field), ('rows', 'cols'))  16.8 us
    ppermute x4, starting transfers between devices, padded_2(): lax.ppermute(tail, axis, [(i, (i + 1) % count) for i in range(ends)])  11.7 us
    ppermute x4, waiting for transfers between devices, padded_2(): lax.ppermute(head, axis, [((i + 1) % count, i) for i in range(ends)])  8.59 us
    ppermute x4, waiting for transfers between devices, padded_2(): lax.ppermute(tail, axis, [(i, (i + 1) % count) for i in range(ends)])  6.85 us
    ppermute x4, starting transfers between devices, padded_2(): lax.ppermute(head, axis, [((i + 1) % count, i) for i in range(ends)])  5.35 us
    dot_general x2, matrix products, row_pass(): jnp.dot(band_matrix(height_out).T, across, precision=lax.Precision.HIGHES...  4.6 us
  transfers between devices with their start and end apart: 9, of which 5 were waited for; matrix products, arithmetic and copies ran while one was open for 14% of the time, Pallas kernels for 0%

commit v1 on v0

--- a/solution.py
+++ b/solution.py
@@ -86,7 +86,7 @@
     )
     weighted = own_weight * log_portions
     cell_count = patch_height * lax.axis_size("rows") * patch_width * lax.axis_size("cols")
-    log_mean = lax.psum(weighted, "hist")
+    log_mean = jnp.sum(lax.all_gather(weighted, "hist"), axis=0)
     mean_field = jnp.exp(log_mean)
     total_mass = lax.psum(jnp.sum(mean_field), ("rows", "cols"))
     barycenter = mean_field * (cell_count / total_mass)

time: 138 us -> 131 us (0.949)
  waiting for transfers between devices: 55.7 us -> 48.7 us
    psum x1 -> x0, waiting for transfers between devices: 40.2 us -> none  [body(): log_mean = lax.psum(weighted, 'hist')]
    all_gather x0 -> x1, waiting for transfers between devices: none -> 33.2 us  [body(): log_mean = jnp.sum(lax.all_gather(weighted, 'hist'), axis=0)]
    reduce_sum x0 -> x1, other arithmetic: none -> 1.84 us  [body(): log_mean = jnp.sum(lax.all_gather(weighted, 'hist'), axis=0)]
where the time goes in v1:
time: 131 us
  waiting for transfers between devices  48.7 us (37%)
  matrix products  24.3 us (19%)
  starting transfers between devices  17 us (13%)
  blocking collectives  16.8 us (13%)
  between operations  16.4 us (13%)
  other arithmetic  5.99 us (5%)
  local copies, waits for them, and re-layouts  1.48 us (1%)
    all_gather x1, waiting for transfers between devices, body(): log_mean = jnp.sum(lax.all_gather(weighted, 'hist'), axis=0)  33.2 us
    dot_general x16, matrix products, column_pass(): jnp.dot(window, band_matrix(span_cols), precision=lax.Precision.HIGHEST,...  19.7 us
    psum x1, blocking collectives, body(): total_mass = lax.psum(jnp.sum(mean_field), ('rows', 'cols'))  16.8 us
    ppermute x4, starting transfers between devices, padded_2(): lax.ppermute(tail, axis, [(i, (i + 1) % count) for i in range(ends)])  11.7 us
    ppermute x4, waiting for transfers between devices, padded_2(): lax.ppermute(head, axis, [((i + 1) % count, i) for i in range(ends)])  8.59 us
    ppermute x4, waiting for transfers between devices, padded_2(): lax.ppermute(tail, axis, [(i, (i + 1) % count) for i in range(ends)])  6.83 us
    ppermute x4, starting transfers between devices, padded_2(): lax.ppermute(head, axis, [((i + 1) % count, i) for i in range(ends)])  5.35 us
    dot_general x2, matrix products, row_pass(): jnp.dot(band_matrix(height_out).T, across, precision=lax.Precision.HIGHES...  4.58 us
  transfers between devices with their start and end apart: 9, of which 5 were waited for; matrix products, arithmetic and copies ran while one was open for 14% of the time, Pallas kernels for 0%

profile of v1, /device:TPU:0, one launch (start us, length us, event | category | flops | bytes accessed | tf_op | source)
XLA Modules:
  0.0 130.7 jit_solution(13227072161378435377)
XLA Ops:
  7.2 0.0 all-gather.3.cloned.1.call-start
  7.2 1.4 %bitcast_exponential_fusion = f32[128,2048]{1,0:T(8,128)S(1)} fusion(f32[1,128,2048]{2,1,0:T(8,128)} %param.4), kind=kLoop, calls=%fused_computation.21 | loop fusion | bytes 2097152 | tf_op jit(solution)/shard_map/exp | solution.py:76
  8.6 5.0 %collective-permute-start = (f32[32,2048]{1,0:T(8,128)S(1)}, f32[32,2048]{1,0:T(8,128)S(1)}, u32[]{:S(2)}, u32[]{:S(2)}) collective-permute-start(f32[32,2048]{1,0:T(8,128)S(1)} %get-tuple-element.12), channel_id=1, source_target_pairs={{0,2},{2,4},{4,6},{1,3},{3,5},{5,7},{8,10},{10,12},{12,14},{9,11},... | collective-permute-start | bytes 786440 | tf_op jit(solution)/shard_map/ppermute | solution.py:18
  13.6 1.3 collective-permute-start.1
  14.9 0.6 fusion.45
  15.6 3.6 %collective-permute-done = f32[32,2048]{1,0:T(8,128)S(1)} collective-permute-done((f32[32,2048]{1,0:T(8,128)S(1)}, f32[32,2048]{1,0:T(8,128)S(1)}, u32[]{:S(2)}, u32[]{:S(2)}) %collective-permute-start) | collective-permute-done | bytes 262176 | tf_op jit(solution)/shard_map/ppermute | solution.py:18
  19.2 4.1 %collective-permute-done.1 = f32[32,2048]{1,0:T(8,128)S(1)} collective-permute-done((f32[32,2048]{1,0:T(8,128)S(1)}, f32[32,2048]{1,0:T(8,128)S(1)}, u32[]{:S(2)}, u32[]{:S(2)}) %collective-permute-start.1) | collective-permute-done | bytes 262176 | tf_op jit(solution)/shard_map/ppermute | solution.py:20
  23.3 0.1 pad_maximum_fusion.28
  23.4 1.3 collective-permute-start.2
  24.7 1.3 collective-permute-start.3
  26.0 0.1 pad_maximum_fusion
  26.1 0.0 collective-permute-done.2
  26.1 1.2 convolution_dynamic-update-slice_fusion.15
  27.4 1.2 convolution_dynamic-update-slice_fusion.14
  28.6 1.2 convolution_dynamic-update-slice_fusion.13
  29.8 1.2 convolution_dynamic-update-slice_fusion.12
  31.0 1.2 convolution_dynamic-update-slice_fusion.11
  32.3 1.2 convolution_dynamic-update-slice_fusion.10
  33.5 1.2 convolution_dynamic-update-slice_fusion.9
  34.7 0.0 copy-start.2
  34.7 0.0 collective-permute-done.3
  34.8 1.3 %convolution_dynamic-update-slice_fusion.8 = f32[192,2048]{1,0:T(8,128)S(1)} fusion(f32[192,2048]{1,0:T(8,128)S(1)} %convolution_dynamic-update-slice_fusion.9, f32[192,32]{1,0:T(8,128)S(1)} %collective-permute-done.3, f32[32,2048]{1,0:T(8,128)S(1)} %collective-permute-done.1, f32[128,2048]{1,0:T(8,128)S(1)} %bitcast_exponential_fusion, ...), kind=kOutput, calls=%fused_computation.12 | convolution fusion | flops 189747200 | bytes 1867780 | tf_op jit(solution)/shard_map/dot_general | solution.py:44
  36.1 0.0 copy-done.2
  36.1 0.0 copy-start.1
  36.1 1.8 %convolution_divide_fusion = f32[128,2048]{1,0:T(8,128)S(1)} fusion(f32[192,2048]{1,0:T(8,128)S(1)} %convolution_dynamic-update-slice_fusion.8, f32[1,128,2048]{2,1,0:T(8,128)S(1)} %copy-done.2, f32[]{:T(128)} %fusion.45), kind=kOutput, calls=%fused_computation.1 | convolution fusion | flops 604487680 | bytes 3670020 | tf_op jit(solution)/shard_map/dot_general | solution.py:55
  37.9 3.5 %collective-permute-start.4 = (f32[32,2048]{1,0:T(8,128)S(1)}, f32[32,2048]{1,0:T(8,128)S(1)}, u32[]{:S(2)}, u32[]{:S(2)}) collective-permute-start(f32[32,2048]{1,0:T(8,128)S(1)} %get-tuple-element.10), channel_id=1, source_target_pairs={{0,2},{2,4},{4,6},{1,3},{3,5},{5,7},{8,10},{10,12},{12,14},{9,11},... | collective-permute-start | bytes 786440 | tf_op jit(solution)/shard_map/ppermute | solution.py:18
  41.4 1.3 collective-permute-start.5
  42.7 0.0 copy-done.1
  42.7 0.6 fusion.123
  44.7 3.2 %collective-permute-done.4 = f32[32,2048]{1,0:T(8,128)S(1)} collective-permute-done((f32[32,2048]{1,0:T(8,128)S(1)}, f32[32,2048]{1,0:T(8,128)S(1)}, u32[]{:S(2)}, u32[]{:S(2)}) %collective-permute-start.4) | collective-permute-done | bytes 262176 | tf_op jit(solution)/shard_map/ppermute | solution.py:18
  47.9 4.5 %collective-permute-done.5 = f32[32,2048]{1,0:T(8,128)S(1)} collective-permute-done((f32[32,2048]{1,0:T(8,128)S(1)}, f32[32,2048]{1,0:T(8,128)S(1)}, u32[]{:S(2)}, u32[]{:S(2)}) %collective-permute-start.5) | collective-permute-done | bytes 262176 | tf_op jit(solution)/shard_map/ppermute | solution.py:20
  52.4 0.1 pad_maximum_fusion.26
  52.5 1.9 %collective-permute-start.6 = (f32[192,32]{1,0:T(8,128)S(1)}, f32[192,32]{1,0:T(8,128)S(1)}, u32[]{:S(2)}, u32[]{:S(2)}) collective-permute-start(f32[192,32]{1,0:T(8,128)S(1)} %get-tuple-element.7), channel_id=1, source_target_pairs={{0,1},{2,3},{4,5},{6,7},{8,9},{10,11},{12,13},{14,15},{16,17},{18,... | collective-permute-start | bytes 73736 | tf_op jit(solution)/shard_map/ppermute | solution.py:18
  54.4 1.5 %collective-permute-start.7 = (f32[192,32]{1,0:T(8,128)S(1)}, f32[192,32]{1,0:T(8,128)S(1)}, u32[]{:S(2)}, u32[]{:S(2)}) collective-permute-start(f32[192,32]{1,0:T(8,128)S(1)} %get-tuple-element.6), channel_id=1, source_target_pairs={{1,0},{3,2},{5,4},{7,6},{9,8},{11,10},{13,12},{15,14},{17,16},{19,... | collective-permute-start | bytes 73736 | tf_op jit(solution)/shard_map/ppermute | solution.py:20
  55.9 0.1 pad_maximum_fusion.1
  56.0 0.0 collective-permute-done.6
  56.0 1.2 convolution_dynamic-update-slice_fusion.7
  57.2 1.2 convolution_dynamic-update-slice_fusion.6
  58.4 1.2 convolution_dynamic-update-slice_fusion.5
  59.7 1.2 convolution_dynamic-update-slice_fusion.4
  60.9 1.2 convolution_dynamic-update-slice_fusion.3
  62.1 1.2 convolution_dynamic-update-slice_fusion.2
  63.3 1.2 convolution_dynamic-update-slice_fusion.1
  64.6 0.0 copy-start
  64.6 0.0 collective-permute-done.7
  64.6 1.3 %convolution_dynamic-update-slice_fusion = f32[192,2048]{1,0:T(8,128)S(1)} fusion(f32[192,2048]{1,0:T(8,128)S(1)} %convolution_dynamic-update-slice_fusion.1, f32[192,32]{1,0:T(8,128)S(1)} %collective-permute-done.7, f32[32,2048]{1,0:T(8,128)S(1)} %collective-permute-done.5, f32[128,2048]{1,0:T(8,128)S(1)} %convolution_divide_fusion, ...), kind=kOutput, calls=%fused_computation.4 | convolution fusion | flops 189747200 | bytes 1867780 | tf_op jit(solution)/shard_map/dot_general | solution.py:44
  65.9 0.0 copy-done
  65.9 2.8 %fusion = (f32[128,2048]{1,0:T(8,128)}, f32[128,2048]{1,0:T(8,128)S(1)}) fusion(f32[1,128,2048]{2,1,0:T(8,128)S(1)} %copy-done, f32[]{:T(128)S(6)} %div.20, f32[192,2048]{1,0:T(8,128)S(1)} %convolution_dynamic-update-slice_fusion, f32[]{:T(128)} %fusion.45), kind=kOutput, calls=%fused_computation.22 | convolution fusion | flops 604749824 | bytes 4718600 | tf_op jit(solution)/shard_map/dot_general | solution.py:55
  68.7 0.0 all-gather.3.cloned.1.call-update
  68.8 33.2 %all-gather.3.cloned.1.call-done = f32[256,2048]{1,0:T(8,128)} async-done(((f32[128,2048]{1,0:T(8,128)}), f32[256,2048]{1,0:T(8,128)}) %all-gather.3.cloned.1.call-update) | async-done | bytes 2097168 | tf_op jit(solution)/shard_map/all_gather | solution.py:89
  102.0 1.8 %reduce_sum.49 = f32[128,2048]{1,0:T(8,128)S(1)} reduce(f32[2,128,2048]{2,1,0:T(8,128)} %bitcast.12, f32[]{:T(128)} %constant.9.clone.1), dimensions={0}, to_apply=%region_3.4 | reduce | flops 262144 | bytes 3145732 | tf_op jit(solution)/shard_map/reduce_sum | solution.py:89
  103.8 0.9 exponential_reduce_fusion
  104.7 16.8 %psum.7 = f32[]{:T(128)} all-reduce(f32[]{:T(128)} %exponential_reduce_fusion), channel_id=1, replica_groups=mesh['groups'=2,'hist'=2,'rows'=4,'cols'=2] {'rows','cols'}, use_global_device_ids=true, to_apply=%region_5.6 | all-reduce | flops 1 | bytes 8 | tf_op jit(solution)/shard_map/psum | solution.py:91
  122.2 1.6 %subtract_bitcast_fusion = (f32[1,128,2048]{2,1,0:T(8,128)}, f32[128,2048]{1,0:T(8,128)}) fusion(f32[128,2048]{1,0:T(8,128)S(1)} %get-tuple-element.15, f32[]{:T(128)S(6)} %div.29, f32[128,2048]{1,0:T(8,128)S(1)} %reduce_sum.49), kind=kLoop, calls=%fused_computation.23 | loop fusion | flops 524288 | bytes 4194308 | tf_op jit(solution)/shard_map/broadcast_in_dim | solution.py:94
  (2 shorter events, 0.1 us)
Async XLA Ops:
  7.2 94.8 %all-gather.3.cloned.1.call-start = ((), (), s32[]{:S(2)}) async-start(), calls=%async_computation | async-start | bytes 3145728 | tf_op jit(solution)/shard_map/all_gather | solution.py:89
  8.6 10.5 %collective-permute-start = (f32[32,2048]{1,0:T(8,128)S(1)}, f32[32,2048]{1,0:T(8,128)S(1)}, u32[]{:S(2)}, u32[]{:S(2)}) collective-permute-start(f32[32,2048]{1,0:T(8,128)S(1)} %get-tuple-element.12), channel_id=1, source_target_pairs={{0,2},{2,4},{4,6},{1,3},{3,5},{5,7},{8,10},{10,12},{12,14},{9,11},... | collective-permute-start | bytes 786440 | tf_op jit(solution)/shard_map/ppermute | solution.py:18
  13.6 9.7 %collective-permute-start.1 = (f32[32,2048]{1,0:T(8,128)S(1)}, f32[32,2048]{1,0:T(8,128)S(1)}, u32[]{:S(2)}, u32[]{:S(2)}) collective-permute-start(f32[32,2048]{1,0:T(8,128)S(1)} %get-tuple-element.13), channel_id=1, source_target_pairs={{2,0},{4,2},{6,4},{3,1},{5,3},{7,5},{10,8},{12,10},{14,12},{11,9},... | collective-permute-start | bytes 786440 | tf_op jit(solution)/shard_map/ppermute | solution.py:20
  23.4 2.8 %collective-permute-start.2 = (f32[192,32]{1,0:T(8,128)S(1)}, f32[192,32]{1,0:T(8,128)S(1)}, u32[]{:S(2)}, u32[]{:S(2)}) collective-permute-start(f32[192,32]{1,0:T(8,128)S(1)} %get-tuple-element.9), channel_id=1, source_target_pairs={{0,1},{2,3},{4,5},{6,7},{8,9},{10,11},{12,13},{14,15},{16,17},{18,... | collective-permute-start | bytes 73736 | tf_op jit(solution)/shard_map/ppermute | solution.py:18
  24.7 10.1 %collective-permute-start.3 = (f32[192,32]{1,0:T(8,128)S(1)}, f32[192,32]{1,0:T(8,128)S(1)}, u32[]{:S(2)}, u32[]{:S(2)}) collective-permute-start(f32[192,32]{1,0:T(8,128)S(1)} %get-tuple-element.8), channel_id=1, source_target_pairs={{1,0},{3,2},{5,4},{7,6},{9,8},{11,10},{13,12},{15,14},{17,16},{19,... | collective-permute-start | bytes 73736 | tf_op jit(solution)/shard_map/ppermute | solution.py:20
  34.7 1.4 %copy-start.2 = (f32[1,128,2048]{2,1,0:T(8,128)S(1)}, f32[1,128,2048]{2,1,0:T(8,128)}, u32[]{:S(2)}) copy-start(f32[1,128,2048]{2,1,0:T(8,128)} %param.3) | copy-start | bytes 3145732
  36.1 6.6 %copy-start.1 = (f32[2]{0:T(128)S(1)}, f32[2]{0:T(128)}, u32[]{:S(2)}) copy-start(f32[2]{0:T(128)} %param.5) | copy-start | bytes 28
  37.9 10.0 %collective-permute-start.4 = (f32[32,2048]{1,0:T(8,128)S(1)}, f32[32,2048]{1,0:T(8,128)S(1)}, u32[]{:S(2)}, u32[]{:S(2)}) collective-permute-start(f32[32,2048]{1,0:T(8,128)S(1)} %get-tuple-element.10), channel_id=1, source_target_pairs={{0,2},{2,4},{4,6},{1,3},{3,5},{5,7},{8,10},{10,12},{12,14},{9,11},... | collective-permute-start | bytes 786440 | tf_op jit(solution)/shard_map/ppermute | solution.py:18
  41.4 11.0 %collective-permute-start.5 = (f32[32,2048]{1,0:T(8,128)S(1)}, f32[32,2048]{1,0:T(8,128)S(1)}, u32[]{:S(2)}, u32[]{:S(2)}) collective-permute-start(f32[32,2048]{1,0:T(8,128)S(1)} %get-tuple-element.11), channel_id=1, source_target_pairs={{2,0},{4,2},{6,4},{3,1},{5,3},{7,5},{10,8},{12,10},{14,12},{11,9},... | collective-permute-start | bytes 786440 | tf_op jit(solution)/shard_map/ppermute | solution.py:20
  52.5 3.5 %collective-permute-start.6 = (f32[192,32]{1,0:T(8,128)S(1)}, f32[192,32]{1,0:T(8,128)S(1)}, u32[]{:S(2)}, u32[]{:S(2)}) collective-permute-start(f32[192,32]{1,0:T(8,128)S(1)} %get-tuple-element.7), channel_id=1, source_target_pairs={{0,1},{2,3},{4,5},{6,7},{8,9},{10,11},{12,13},{14,15},{16,17},{18,... | collective-permute-start | bytes 73736 | tf_op jit(solution)/shard_map/ppermute | solution.py:18
  54.4 10.2 %collective-permute-start.7 = (f32[192,32]{1,0:T(8,128)S(1)}, f32[192,32]{1,0:T(8,128)S(1)}, u32[]{:S(2)}, u32[]{:S(2)}) collective-permute-start(f32[192,32]{1,0:T(8,128)S(1)} %get-tuple-element.6), channel_id=1, source_target_pairs={{1,0},{3,2},{5,4},{7,6},{9,8},{11,10},{13,12},{15,14},{17,16},{19,... | collective-permute-start | bytes 73736 | tf_op jit(solution)/shard_map/ppermute | solution.py:20
  64.6 1.4 %copy-start = (f32[1,128,2048]{2,1,0:T(8,128)S(1)}, f32[1,128,2048]{2,1,0:T(8,128)}, u32[]{:S(2)}) copy-start(f32[1,128,2048]{2,1,0:T(8,128)} %param.4) | copy-start | bytes 3145732
Sparse Core Ops, SparseCore 0:
  68.9 33.0 all-gather.2
